TPU v7x, 32 devices: a whole 2x2x4 slice. The times are simulated.
32 devices in a mesh: groups: 2 (over x), tier: 16 (over z, y, core).
Axes of the slice: x: 2, y: 2, z: 4, core: 2. Of those that a mesh axis runs over, the one named last changes fastest.
Arguments:
- rho: float32 [256, 2, 256, 256], P(('groups', 'tier')), parts along dimension 0, may hold values from -6 to 6
- hamiltonian: float32 [256, 256], replicated, may hold values from -0.375 to 0.375
- couplings: float32 [4, 256, 256], replicated, may hold values from -0.375 to 0.375
- bath_coef: float32 [8, 2], P('groups'), parts along dimension 0, may hold values from 0.3 to 1.5
- damping: float32 [256], P(('groups', 'tier')), parts along dimension 0, may hold values from 0.2 to 3
- match_edges: int32 [16, 4, 1, 5], P('tier'), may hold values from 0 to 7, as said below
- left_rows: int32 [16, 6, 5], replicated, may hold values from 0 to 127, as said below
- left_count: int32 [16], replicated, may hold values from 1 to 6, as said below
Outputs:
- rho_next: float32 [256, 2, 256, 256], P(('groups', 'tier')), parts along dimension 0
There are 2 independent parts, one for each index of `groups`. A program takes and returns all parts, laid end to end along the dimension named above; an argument that names none is the same for every part. Nothing has to cross between parts.
Inputs may be any that keep to these rules, and one draw needn't show every extreme that they name: match_edges[b, c, j] = (target slot, partner slot, mode, lower flag 0 or 1, occupation 1 to 3); the row (b XOR 2^c, c, j) describes the same edge from the partner's side: its target slot is this row's partner slot and the reverse, same mode and occupation, opposite lower flag. left_rows[b, j] = (target slot, source matrix index, mode, lower flag 0 or 1, occupation 1 to 3); the source's block lies at cyclic block distance 1 to 4 from b, and the rows of one block name distinct source blocks. Only the first left_count[b] rows of block b are live; some block has exactly 6.
All inputs are finite; a program needn't handle non-finite values.
Results may differ from a plain program's by a relative error of at most 0.00005.
Values sent between devices are 32-bit elements; how exact they have to be, the bound alone decides.
A program may use at most 128 MiB of HBM per device.

v0:
```python
import functools

import jax
import jax.numpy as jnp
from jax import lax
from jax.experimental import pallas as pl
from jax.experimental.pallas import tpu as pltpu
from jax.sharding import PartitionSpec as P

REACH = 4
STEP = 0.1
F32 = jnp.float32
BF16 = jnp.bfloat16


def split(value):
    high = value.astype(BF16)
    low = (value - high.astype(F32)).astype(BF16)
    return high, low


def flip(index, stride):
    return index + stride - 2 * stride * ((index // stride) % 2)


def kernel(
    tier_size,
    colours,
    rho_any,
    ham_any,
    coup_any,
    bath_ref,
    damp_ref,
    match_ref,
    left_ref,
    count_ref,
    out_ref,
    rho_ref,
    ham_ref,
    coup_ref,
    load_sem,
    first_ref,
    term_ref,
    packed,
    arrived,
    op_left,
    op_right,
    send_sem,
    recv_sem,
):
    loads = [
        pltpu.make_async_copy(rho_any, rho_ref, load_sem.at[0]),
        pltpu.make_async_copy(ham_any, ham_ref, load_sem.at[1]),
        pltpu.make_async_copy(coup_any, coup_ref, load_sem.at[2]),
    ]
    for load in loads:
        load.start()
    me = lax.axis_index("tier")
    mats = rho_ref.shape[0]
    order = rho_ref.shape[2]
    modes = coup_ref.shape[0]
    left_cap = left_ref.shape[1]
    deltas = [d for d in range(REACH, 0, -1)] + [d for d in range(-1, -REACH - 1, -1)]
    rows = colours + len(deltas)

    targets = [flip(me, 2**c) for c in range(colours)]
    targets += [lax.rem(me - d + tier_size, tier_size) for d in deltas]

    barrier = pltpu.get_barrier_semaphore()
    for device in targets:
        pl.semaphore_signal(barrier, inc=1, device_id={"tier": device}, device_id_type=pl.DeviceIdType.MESH)
    pl.semaphore_wait(barrier, rows)

    def asked_slot(delta):
        asker = lax.rem(me - delta + tier_size, tier_size)
        slot = jnp.int32(0)
        for j in range(left_cap):
            source = left_ref[1, j, asker]
            hit = (source // mats == me) & (j < count_ref[asker])
            slot = jnp.where(hit, source % mats, slot)
        return slot

    slots = [match_ref[c, 0] for c in range(colours)] + [asked_slot(d) for d in deltas]

    def copies(stage):
        return [
            pltpu.make_async_remote_copy(
                src_ref=packed.at[i],
                dst_ref=arrived.at[stage, i],
                send_sem=send_sem.at[stage, i],
                recv_sem=recv_sem.at[stage, i],
                device_id={"tier": targets[i]},
                device_id_type=pl.DeviceIdType.MESH,
            )
            for i in range(rows)
        ]

    def products(value, left, right):
        re_high, re_low = split(value[0])
        im_high, im_low = split(value[1])
        column = jnp.concatenate(
            [
                jnp.concatenate([re_high, re_low, re_high], axis=0),
                jnp.concatenate([im_high, im_low, im_high], axis=0),
            ],
            axis=1,
        )
        row = jnp.concatenate(
            [
                jnp.concatenate([re_high, re_low, re_high], axis=1),
                jnp.concatenate([im_high, im_low, im_high], axis=1),
            ],
            axis=0,
        )
        p = jnp.dot(left, column, preferred_element_type=F32)
        r = jnp.dot(row, right, preferred_element_type=F32)
        return p[:, :order], p[:, order:], r[:order], r[order:]

    def row_facts(i):
        c = jnp.minimum(i, colours - 1)
        is_match = i < colours
        q = i - colours
        delta = jnp.where(q < REACH, REACH - q, REACH - 1 - q)
        source = lax.rem(me + delta + tier_size, tier_size)
        target, mode, flag, occ, weight = jnp.int32(0), jnp.int32(0), jnp.int32(0), jnp.int32(0), jnp.int32(0)
        for j in range(left_cap):
            hit = (left_ref[1, j, me] // mats == source) & (j < count_ref[me])
            target = jnp.where(hit, left_ref[0, j, me], target)
            mode = jnp.where(hit, left_ref[2, j, me], mode)
            flag = jnp.where(hit, left_ref[3, j, me], flag)
            occ = jnp.where(hit, left_ref[4, j, me], occ)
            weight = jnp.where(hit, 1, weight)
        target = jnp.where(is_match, match_ref[c, 0], target)
        mode = jnp.where(is_match, match_ref[c, 2], mode)
        flag = jnp.where(is_match, match_ref[c, 3], flag)
        occ = jnp.where(is_match, match_ref[c, 4], occ)
        weight = jnp.where(is_match, 1, weight)
        a = jnp.where(flag == 1, F32(1.0), bath_ref[0, mode])
        b = jnp.where(flag == 1, F32(0.0), bath_ref[1, mode])
        return target, mode, a, b, occ, weight

    def handle_row(i, stage, scale, acc):
        pltpu.make_async_remote_copy(
            src_ref=packed.at[i],
            dst_ref=arrived.at[stage, i],
            send_sem=send_sem.at[stage, i],
            recv_sem=recv_sem.at[stage, i],
            device_id={"tier": targets[0]},
            device_id_type=pl.DeviceIdType.MESH,
        ).wait_recv()
        target, mode, a, b, occ, weight = row_facts(i)
        p_re, p_im, r_re, r_im = products(arrived[stage, i], op_left[mode], op_right[mode])
        root = jnp.sqrt(jnp.full((1, order), occ, jnp.int32).astype(F32)) * weight.astype(F32) * scale
        ca = root * a
        cb = root * b
        term_ref[0] = ca * (p_im - r_im) + cb * (p_re + r_re)
        term_ref[1] = cb * (p_im + r_im) - ca * (p_re - r_re)

        def add(s, carry):
            chosen = jnp.where(target == s, F32(1.0), F32(0.0))
            acc[s] = acc[s] + chosen * term_ref[...]
            return carry

        lax.fori_loop(0, mats, add, 0)

    def pack_and_send(source, stage):
        sends = copies(stage)
        for i in range(rows):
            packed[i] = source[slots[i]]
            if i > 0:
                sends[i - 1].start()
        sends[rows - 1].start()
        return sends

    loads[0].wait()
    sends = pack_and_send(rho_ref, 0)
    loads[1].wait()
    loads[2].wait()

    def prepare(k, carry):
        high, low = split(coup_ref[k])
        op_left[k] = jnp.concatenate([high, high, low], axis=1)
        op_right[k] = jnp.concatenate([high, high, low], axis=0)
        return carry

    lax.fori_loop(0, modes, prepare, 0)
    high, low = split(ham_ref[...])
    op_left[modes] = jnp.concatenate([high, high, low], axis=1)
    op_right[modes] = jnp.concatenate([high, high, low], axis=0)

    def own(n, carry):
        value = rho_ref[n]
        p_re, p_im, r_re, r_im = products(value, op_left[modes], op_right[modes])
        first_ref[n, 0] = (p_im - r_im) - damp_ref[n] * value[0]
        first_ref[n, 1] = (r_re - p_re) - damp_ref[n] * value[1]
        return carry

    lax.fori_loop(0, mats, own, 0)

    def row_first(i, carry):
        handle_row(i, 0, F32(1.0), first_ref)
        return carry

    lax.fori_loop(0, rows, row_first, 0)
    for copy in sends:
        copy.wait_send()

    sends = pack_and_send(first_ref, 1)

    half = F32(0.5 * STEP * STEP)

    def own_second(n, carry):
        value = first_ref[n]
        p_re, p_im, r_re, r_im = products(value, op_left[modes], op_right[modes])
        out_ref[n, 0] = rho_ref[n, 0] + F32(STEP) * value[0] + half * ((p_im - r_im) - damp_ref[n] * value[0])
        out_ref[n, 1] = rho_ref[n, 1] + F32(STEP) * value[1] + half * ((r_re - p_re) - damp_ref[n] * value[1])
        return carry

    lax.fori_loop(0, mats, own_second, 0)

    def row_second(i, carry):
        handle_row(i, 1, half, out_ref)
        return carry

    lax.fori_loop(0, rows, row_second, 0)
    for copy in sends:
        copy.wait_send()


def body(tier_size, rho, hamiltonian, couplings, bath_coef, damping, match_edges, left_rows, left_count):
    mats, _, order, _ = rho.shape
    modes = couplings.shape[0]
    table = match_edges.reshape(-1, match_edges.shape[-1])
    colours = table.shape[0]
    rows = colours + 2 * REACH
    vmem = pl.BlockSpec(memory_space=pltpu.VMEM)
    hbm = pl.BlockSpec(memory_space=pl.ANY)
    smem = pl.BlockSpec(memory_space=pltpu.SMEM)
    return pl.pallas_call(
        functools.partial(kernel, tier_size, colours),
        out_shape=pltpu.VMEM(rho.shape, F32),
        in_specs=[hbm, hbm, hbm, smem, smem, smem, smem, smem],
        out_specs=vmem,
        scratch_shapes=[
            pltpu.VMEM(rho.shape, F32),
            pltpu.VMEM(hamiltonian.shape, F32),
            pltpu.VMEM(couplings.shape, F32),
            pltpu.SemaphoreType.DMA((3,)),
            pltpu.VMEM(rho.shape, F32),
            pltpu.VMEM((2, order, order), F32),
            pltpu.VMEM((rows, 2, order, order), F32),
            pltpu.VMEM((2, rows, 2, order, order), F32),
            pltpu.VMEM((modes + 1, order, 3 * order), BF16),
            pltpu.VMEM((modes + 1, 3 * order, order), BF16),
            pltpu.SemaphoreType.DMA((2, rows)),
            pltpu.SemaphoreType.DMA((2, rows)),
        ],
        compiler_params=pltpu.CompilerParams(
            collective_id=0, has_side_effects=True, vmem_limit_bytes=50 * 1024 * 1024
        ),
    )(rho, hamiltonian, couplings, bath_coef.T, damping, table, left_rows.transpose(2, 1, 0), left_count)


def solution(mesh):
    placed = (
        P(("groups", "tier"), None, None, None),
        P(),
        P(),
        P("groups", None),
        P(("groups", "tier")),
        P("tier", None, None, None),
        P(),
        P(),
    )
    return jax.shard_map(
        functools.partial(body, mesh.shape["tier"]),
        mesh=mesh,
        in_specs=placed,
        out_specs=P(("groups", "tier"), None, None, None),
        check_vma=False,
    )
```

profile of v0, /device:TPU:1, one launch (start us, length us, event | category | flops | bytes accessed | tf_op | source)
XLA Modules:
  0.0 170.7 jit_solution(12137388400223671506)
XLA Ops:
  0.0 168.6 %shard_map.82 = f32[8,2,256,256]{3,2,1,0:T(8,128)S(1)} custom-call(f32[8,2,256,256]{3,2,1,0:T(8,128)} %rho_any.1, f32[256,256]{1,0:T(8,128)} %ham_any.1, f32[4,256,256]{2,1,0:T(8,128)} %coup_any.1, f32[2,4]{1,0:T(2,128)} %bitcast.5, f32[8]{0:T(128)} %damp_ref.1, s32[4,5]{1,0:T(4,128)} %bitcast.4, s32[5,6,16]{2,1,0:T(8,128)} %bitcast.3, s32[16]{0:T(128)} %count_ref.1), custom_call_target="tpu_custom_call" | custom-call | tf_op jit(solution)/shard_map/pallas_call | solution.py:239
  168.7 2.0 %copy.10 = f32[8,2,256,256]{3,2,1,0:T(8,128)} copy(f32[8,2,256,256]{3,2,1,0:T(8,128)S(1)} %shard_map.82) | data formatting | bytes 8388608
where the time goes:
time: 171 us
  Pallas kernels  169 us (99%)
  local copies, waits for them, and re-layouts  2.02 us (1%)
    pallas_call x1, Pallas kernels, body(): pl.pallas_call(functools.partial(kernel, tier_size, colours), out_shape=p...  169 us

commit v1 on v0

v1 whole, which is shorter than its diff:
```python
import functools

import jax
import jax.numpy as jnp
from jax import lax
from jax.experimental import pallas as pl
from jax.experimental.pallas import tpu as pltpu
from jax.sharding import PartitionSpec as P

REACH = 4
STEP = 0.1
F32 = jnp.float32
BF16 = jnp.bfloat16
I32 = jnp.int32

SLOT = (1, 63)
TARGET = (7, 63)
MODE = (13, 31)
FLAG = (18, 1)
OCC = (19, 15)
CORE = (23, 1)
PLACE = (24, 3)

HEAVY = ((2, 0), (2, 1), (3, 0), (3, 1), (2, 2), (3, 2), (3, 3))
LIGHT = ((2, 2), (2, 3), (3, 3))
CROSSING = 4

VARIANTS = ((3, 2, 3), (4, 2, 3), (5, 3, 3), (7, 3, 4))


def split(value):
    high = value.astype(BF16)
    low = (value - high.astype(F32)).astype(BF16)
    return high, low


def flip(index, stride):
    return index + stride - 2 * stride * ((index // stride) % 2)


def put(field, value):
    return value << field[0]


def get(field, code):
    return (code >> field[0]) & field[1]


def distance_index(source, target, tier_size):
    d = lax.rem(source - target + tier_size, tier_size)
    return jnp.where(d <= REACH, d - 1, d - tier_size + 2 * REACH)


def plan_kernel(tier_size, mats, left_ref, count_ref, pair_ref, heavy_ref, light_ref, pick_ref):
    left_cap = left_ref.shape[1]
    places = 2 * REACH

    def clear(ref):
        def one(i, carry):
            ref[i] = jnp.int32(0)
            return carry

        lax.fori_loop(0, ref.shape[0], one, 0)

    clear(pair_ref)
    clear(heavy_ref)
    clear(light_ref)

    def block(b, carry):
        count = count_ref[b]
        for j in range(left_cap):
            source = left_ref[1, j, b]
            owner = lax.div(source, jnp.int32(mats))
            code = 1 + put(SLOT, source - owner * mats) + put(TARGET, left_ref[0, j, b])
            code = code + put(MODE, left_ref[2, j, b]) + put(FLAG, left_ref[3, j, b]) + put(OCC, left_ref[4, j, b])
            index = jnp.clip(distance_index(owner, b, tier_size), 0, places - 1)
            pair_ref[jnp.where(j < count, b * places + index, tier_size * places)] = code
        return carry

    lax.fori_loop(0, tier_size, block, 0)

    def chip(k, most):
        plane, half = k // 2, k % 2
        toward = 2 * half - 1

        def place(m):
            return jnp.where(half == 1, m, REACH - 1 - m)

        def fill(ref, width, pairs, step):
            other = lax.rem(plane + step + tier_size // REACH, tier_size // REACH)
            rank = jnp.int32(0)
            ranks = []
            for m_source, m_target in pairs:
                source = plane * REACH + place(m_source)
                target = other * REACH + place(m_target)
                code = pair_ref[target * places + distance_index(source, target, tier_size)]
                ref[k * width + rank] = code + put(CORE, source % 2) + put(PLACE, place(m_target))
                rank = rank + (code & 1)
                ranks.append(rank)
            ref[k * width + rank] = jnp.int32(0)
            return ranks

        heavy = fill(heavy_ref, 8, HEAVY, toward)
        light = fill(light_ref, 4, LIGHT, -toward)
        found = (heavy[-1], light[-1], heavy[CROSSING - 1])
        return tuple(jnp.maximum(x, y) for x, y in zip(most, found))

    most = lax.fori_loop(0, tier_size // 2, chip, (jnp.int32(0),) * 3)
    pick = jnp.int32(len(VARIANTS) - 1)
    for i in reversed(range(len(VARIANTS) - 1)):
        a, b, e = VARIANTS[i]
        pick = jnp.where((most[0] <= a) & (most[1] <= b) & (most[2] <= e), i, pick)
    pick_ref[0] = pick


def row_order(variant, colours):
    a, b, e = variant
    timed = [(1.0 + i, 0, "heavy", i) for i in range(a)]
    timed += [(1.2 + i, 1, "light", i) for i in range(b)]
    timed += [(3.1 + i, 2, "cross", i) for i in range(e)]
    lanes = [(kind, i) for _, _, kind, i in sorted(timed)]
    return [("plane", 0), ("plane", 1), ("colour", 1)] + lanes + [("colour", c) for c in range(2, colours)]


def kernel(
    tier_size,
    colours,
    variant,
    rho_any,
    ham_any,
    coup_any,
    bath_ref,
    damp_ref,
    match_ref,
    pair_ref,
    heavy_ref,
    light_ref,
    out_ref,
    rho_ref,
    ham_ref,
    coup_ref,
    load_sem,
    first_ref,
    term_ref,
    share_mine,
    share_other,
    packed,
    lanes,
    arrived,
    op_left,
    op_right,
    fact,
    share_send,
    share_recv,
    send_sem,
    recv_sem,
):
    loads = [
        pltpu.make_async_copy(rho_any, rho_ref, load_sem.at[0]),
        pltpu.make_async_copy(ham_any, ham_ref, load_sem.at[1]),
        pltpu.make_async_copy(coup_any, coup_ref, load_sem.at[2]),
    ]
    for load in loads:
        load.start()
    me = lax.axis_index("tier")
    mats = rho_ref.shape[0]
    order = rho_ref.shape[2]
    modes = coup_ref.shape[0]
    places = 2 * REACH
    a_lanes, b_lanes, e_lanes = variant
    rows = row_order(variant, colours)
    index_of = {row: i for i, row in enumerate(rows)}
    first_lane = 3
    last_lane = first_lane + a_lanes + b_lanes + e_lanes

    core = me % 2
    place = me % REACH
    half = place // 2
    toward = 2 * half - 1
    mate = flip(me, 1)
    across = flip(me, 2)
    beside = [across - core, across - core + 1]
    heavy_to = lax.rem(me + REACH * toward + tier_size, tier_size)
    light_to = lax.rem(me - REACH * toward + tier_size, tier_size)
    partners = [flip(me, 2**c) for c in range(colours)]

    greeted = [mate, beside[0], beside[1], heavy_to, light_to] + partners[2:]
    barrier = pltpu.get_barrier_semaphore()
    for device in greeted:
        pl.semaphore_signal(barrier, inc=1, device_id={"tier": device}, device_id_type=pl.DeviceIdType.MESH)
    pl.semaphore_wait(barrier, len(greeted))

    def remote(source, target, send, recv, device):
        return pltpu.make_async_remote_copy(
            src_ref=source,
            dst_ref=target,
            send_sem=send,
            recv_sem=recv,
            device_id={"tier": device},
            device_id_type=pl.DeviceIdType.MESH,
        )

    def pair_code(source, target):
        return pair_ref[target * places + distance_index(source, target, tier_size)]

    def match_code(c):
        return (
            1
            + put(TARGET, match_ref[c, 0])
            + put(SLOT, match_ref[c, 1])
            + put(MODE, match_ref[c, 2])
            + put(FLAG, match_ref[c, 3])
            + put(OCC, match_ref[c, 4])
        )

    def mine(code):
        return jnp.where(get(PLACE, code) == place, code, 0)

    heavy_from = light_to // 2
    light_from = heavy_to // 2
    cross_from = lax.rem(across + REACH * toward + tier_size, tier_size) // 2
    for i, (kind, number) in enumerate(rows):
        if kind == "plane":
            fact[i] = pair_code(beside[number], me)
        elif kind == "colour":
            fact[i] = match_code(number)
        elif kind == "heavy":
            fact[i] = mine(heavy_ref[heavy_from * 8 + number])
        elif kind == "light":
            fact[i] = mine(light_ref[light_from * 4 + number])
        else:
            fact[i] = mine(heavy_ref[cross_from * 8 + number])
    near = len(rows)
    fact[near] = match_code(0)
    fact[near + 1] = pair_code(mate, me)

    direct = [("colour", c) for c in range(colours - 1, 1, -1)] + [("colour", 1), ("plane", 0), ("plane", 1)]
    direct_to = partners[colours - 1 : 1 : -1] + [across] + beside
    far = len(direct) - 3

    def direct_slot(n):
        kind, number = direct[n]
        if kind == "colour":
            return match_ref[number, 0]
        return get(SLOT, pair_code(me, beside[number]))

    def direct_copy(n, stage, part):
        kind, number = direct[n]
        row = core if kind == "plane" else index_of[direct[n]]
        return remote(
            packed.at[n, part],
            arrived.at[stage, row, part],
            send_sem.at[stage, n, part],
            recv_sem.at[stage, row, part],
            direct_to[n],
        )

    outgoing = [("heavy", i) for i in range(a_lanes)] + [("light", i) for i in range(b_lanes)]
    outgoing = [row for row in rows if row in outgoing]

    def lane_copy(n, stage):
        row = index_of[outgoing[n]]
        return remote(
            lanes.at[n],
            arrived.at[stage, row, core],
            send_sem.at[stage, len(direct) + n, 0],
            recv_sem.at[stage, row, core],
            heavy_to if outgoing[n][0] == "heavy" else light_to,
        )

    def mate_copy(row, stage):
        return remote(
            arrived.at[stage, row, core],
            arrived.at[stage, row, core],
            send_sem.at[stage, len(direct) + row, 1],
            recv_sem.at[stage, row, core],
            mate,
        )

    def cross_copy(row, stage):
        landing = index_of[("cross", rows[row][1])]
        return remote(
            arrived.at[stage, row, core],
            arrived.at[stage, landing, core],
            send_sem.at[stage, len(direct) + row, 2],
            recv_sem.at[stage, landing, core],
            across,
        )

    def share_copies(source, stage):
        return [
            remote(source.at[:, 1 - core], share_mine.at[stage], share_send.at[stage, 0], share_recv.at[stage, 0], mate),
            remote(source.at[:, core], share_other.at[stage], share_send.at[stage, 1], share_recv.at[stage, 1], mate),
        ]

    def wait_part(row, part, stage):
        remote(
            arrived.at[stage, row, part],
            arrived.at[stage, row, part],
            send_sem.at[stage, 0, 0],
            recv_sem.at[stage, row, part],
            mate,
        ).wait_recv()

    def hand_on(row, stage):
        kind, number = rows[row]
        wait_part(row, core, stage)
        mate_copy(row, stage).start()
        if kind == "heavy" and number < e_lanes:
            cross_copy(row, stage).start()

    def products(value, left, right):
        re_high, re_low = split(value[0])
        im_high, im_low = split(value[1])
        column = jnp.concatenate(
            [
                jnp.concatenate([re_high, re_low, re_high], axis=0),
                jnp.concatenate([im_high, im_low, im_high], axis=0),
            ],
            axis=1,
        )
        row = jnp.concatenate(
            [
                jnp.concatenate([re_high, re_low, re_high], axis=1),
                jnp.concatenate([im_high, im_low, im_high], axis=1),
            ],
            axis=0,
        )
        p = jnp.dot(left, column, preferred_element_type=F32)
        r = jnp.dot(row, right, preferred_element_type=F32)
        return p[:, :order], p[:, order:], r[:order], r[order:]

    def add_row(code, value, scale, acc):
        weight, target, mode, occ = code & 1, get(TARGET, code), get(MODE, code), get(OCC, code)
        lower = get(FLAG, code) == 1
        a = jnp.where(lower, F32(1.0), bath_ref[0, mode])
        b = jnp.where(lower, F32(0.0), bath_ref[1, mode])
        p_re, p_im, r_re, r_im = products(value, op_left[mode], op_right[mode])
        root = jnp.sqrt(jnp.full((1, order), occ, I32).astype(F32)) * weight.astype(F32) * scale
        ca = root * a
        cb = root * b
        term_ref[0] = ca * (p_im - r_im) + cb * (p_re + r_re)
        term_ref[1] = cb * (p_im + r_im) - ca * (p_re - r_re)

        def add(s, carry):
            chosen = jnp.where(target == s, F32(1.0), F32(0.0))
            acc[s] = acc[s] + chosen * term_ref[...]
            return carry

        lax.fori_loop(0, mats, add, 0)

    def stage_rows(stage, source, scale, acc, own):
        shares = share_copies(source, stage)

        started = []
        for n in range(len(direct)):
            packed[n] = source[direct_slot(n)]
            if n == 1:
                direct_copy(0, stage, 0).start()
                shares[0].start()
            elif n > 1:
                for part in range(1 if n - 1 < far else 2):
                    direct_copy(n - 1, stage, part).start()
        for part in range(2):
            direct_copy(len(direct) - 1, stage, part).start()
        shares[1].start()

        own()

        shares[0].wait_recv()
        for n, row in enumerate(outgoing):
            if row[0] == "heavy":
                code = heavy_ref[(me // 2) * 8 + row[1]]
            else:
                code = light_ref[(me // 2) * 4 + row[1]]
            slot = get(SLOT, code)
            lanes[n] = jnp.where(get(CORE, code) == core, source[slot, core], share_mine[stage, slot])
            if n > 0:
                lane_copy(n - 1, stage).start()
        lane_copy(len(outgoing) - 1, stage).start()
        for n in range(far - 1, -1, -1):
            direct_copy(n, stage, 1).start()

        shares[1].wait_recv()

        def near_row(i, carry):
            code = fact[near + i]
            slot = get(SLOT, code)
            my_part = share_mine[stage, slot]
            other_part = share_other[stage, slot]
            is_real = core == 0
            value = (jnp.where(is_real, my_part, other_part), jnp.where(is_real, other_part, my_part))
            add_row(code, value, scale, acc)
            return carry

        lax.fori_loop(0, 2, near_row, 0)

        def row_step(i, carry):
            for row in range(first_lane, last_lane):
                @pl.when(i == row - 1)
                def _():
                    hand_on(row, stage)

            wait_part(i, 1 - core, stage)

            @pl.when((i < first_lane) | (i >= last_lane))
            def _():
                wait_part(i, core, stage)

            add_row(fact[i], arrived[stage, i], scale, acc)
            return carry

        lax.fori_loop(0, len(rows), row_step, 0)

        for share in shares:
            share.wait_send()
        for n in range(len(direct)):
            for part in range(2):
                direct_copy(n, stage, part).wait_send()
        for n in range(len(outgoing)):
            lane_copy(n, stage).wait_send()
        for row in range(first_lane, last_lane):
            mate_copy(row, stage).wait_send()
            kind, number = rows[row]
            if kind == "heavy" and number < e_lanes:
                cross_copy(row, stage).wait_send()

    def own_first():
        loads[1].wait()
        loads[2].wait()

        def prepare(k, carry):
            high, low = split(coup_ref[k])
            op_left[k] = jnp.concatenate([high, high, low], axis=1)
            op_right[k] = jnp.concatenate([high, high, low], axis=0)
            return carry

        lax.fori_loop(0, modes, prepare, 0)
        high, low = split(ham_ref[...])
        op_left[modes] = jnp.concatenate([high, high, low], axis=1)
        op_right[modes] = jnp.concatenate([high, high, low], axis=0)

        def own(n, carry):
            value = rho_ref[n]
            p_re, p_im, r_re, r_im = products(value, op_left[modes], op_right[modes])
            first_ref[n, 0] = (p_im - r_im) - damp_ref[n] * value[0]
            first_ref[n, 1] = (r_re - p_re) - damp_ref[n] * value[1]
            return carry

        lax.fori_loop(0, mats, own, 0)

    factor = F32(0.5 * STEP * STEP)

    def own_second():
        def own(n, carry):
            value = first_ref[n]
            p_re, p_im, r_re, r_im = products(value, op_left[modes], op_right[modes])
            out_ref[n, 0] = rho_ref[n, 0] + F32(STEP) * value[0] + factor * ((p_im - r_im) - damp_ref[n] * value[0])
            out_ref[n, 1] = rho_ref[n, 1] + F32(STEP) * value[1] + factor * ((r_re - p_re) - damp_ref[n] * value[1])
            return carry

        lax.fori_loop(0, mats, own, 0)

    loads[0].wait()
    stage_rows(0, rho_ref, F32(1.0), first_ref, own_first)
    stage_rows(1, first_ref, factor, out_ref, own_second)


def body(tier_size, rho, hamiltonian, couplings, bath_coef, damping, match_edges, left_rows, left_count):
    mats, _, order, _ = rho.shape
    modes = couplings.shape[0]
    table = match_edges.reshape(-1, match_edges.shape[-1])
    colours = table.shape[0]
    vmem = pl.BlockSpec(memory_space=pltpu.VMEM)
    hbm = pl.BlockSpec(memory_space=pl.ANY)
    smem = pl.BlockSpec(memory_space=pltpu.SMEM)

    pair, heavy, light, pick = pl.pallas_call(
        functools.partial(plan_kernel, tier_size, mats),
        out_shape=[
            jax.ShapeDtypeStruct((tier_size * 2 * REACH + 1,), I32),
            jax.ShapeDtypeStruct((tier_size // 2 * 8,), I32),
            jax.ShapeDtypeStruct((tier_size // 2 * 4,), I32),
            jax.ShapeDtypeStruct((1,), I32),
        ],
        in_specs=[smem, smem],
        out_specs=[smem] * 4,
    )(left_rows.transpose(2, 1, 0), left_count)

    def step(number, variant):
        a, b, e = variant
        rows = len(row_order(variant, colours))
        direct = colours + 1
        return pl.pallas_call(
            functools.partial(kernel, tier_size, colours, variant),
            out_shape=pltpu.VMEM(rho.shape, F32),
            in_specs=[hbm, hbm, hbm] + [smem] * 6,
            out_specs=vmem,
            scratch_shapes=[
                pltpu.VMEM(rho.shape, F32),
                pltpu.VMEM(hamiltonian.shape, F32),
                pltpu.VMEM(couplings.shape, F32),
                pltpu.SemaphoreType.DMA((3,)),
                pltpu.VMEM(rho.shape, F32),
                pltpu.VMEM((2, order, order), F32),
                pltpu.VMEM((2, mats, order, order), F32),
                pltpu.VMEM((2, mats, order, order), F32),
                pltpu.VMEM((direct, 2, order, order), F32),
                pltpu.VMEM((a + b, order, order), F32),
                pltpu.VMEM((2, rows, 2, order, order), F32),
                pltpu.VMEM((modes + 1, order, 3 * order), BF16),
                pltpu.VMEM((modes + 1, 3 * order, order), BF16),
                pltpu.SMEM((rows + 2,), I32),
                pltpu.SemaphoreType.DMA((2, 2)),
                pltpu.SemaphoreType.DMA((2, 2)),
                pltpu.SemaphoreType.DMA((2, direct + rows, 3)),
                pltpu.SemaphoreType.DMA((2, rows, 2)),
            ],
            compiler_params=pltpu.CompilerParams(
                collective_id=number, has_side_effects=True, vmem_limit_bytes=58 * 1024 * 1024
            ),
        )

    return lax.switch(
        pick[0],
        [step(i, variant) for i, variant in enumerate(VARIANTS)],
        rho,
        hamiltonian,
        couplings,
        bath_coef.T,
        damping,
        table,
        pair,
        heavy,
        light,
    )


def solution(mesh):
    placed = (
        P(("groups", "tier"), None, None, None),
        P(),
        P(),
        P("groups", None),
        P(("groups", "tier")),
        P("tier", None, None, None),
        P(),
        P(),
    )
    return jax.shard_map(
        functools.partial(body, mesh.shape["tier"]),
        mesh=mesh,
        in_specs=placed,
        out_specs=P(("groups", "tier"), None, None, None),
        check_vma=False,
    )
```

time: 171 us -> 136 us (0.80); the launches traced: 171 us -> 138 us
  Pallas kernels: 169 us -> 136 us
    pallas_call x1 -> x2, Pallas kernels: 169 us -> 136 us  [the longest x1 130 us: body(): lax.switch(pick[0], [step(i, variant) for i, variant in enumerate(VARIANT...]
where the time goes in v1:
time: 136 us; the launch traced here: 138 us
  Pallas kernels  136 us (100%)
  local copies, waits for them, and re-layouts  2.02 us (1%)
    pallas_call x1, Pallas kernels, body(): lax.switch(pick[0], [step(i, variant) for i, variant in enumerate(VARIANT...  130 us
    pallas_call x1, Pallas kernels, body(): pl.pallas_call(functools.partial(plan_kernel, tier_size, mats), out_shape...  5.24 us

profile of v1, /device:TPU:1, one launch (start us, length us, event | category | flops | bytes accessed | tf_op | source)
XLA Modules:
  0.0 138.5 jit_solution(8740758040652667982)
XLA Ops:
  0.0 5.2 %shard_map.106 = (s32[129]{0:T(256)S(1)}, s32[64]{0:T(128)S(1)}, s32[32]{0:T(128)S(1)}, s32[1]{0:T(128)}) custom-call(s32[5,6,16]{2,1,0:T(8,128)} %bitcast.19, s32[16]{0:T(128)} %count_ref.1), custom_call_target="tpu_custom_call" | custom-call | tf_op jit(solution)/shard_map/pallas_call | solution.py:478
  5.9 130.6 %conditional.1 = (f32[8,2,256,256]{3,2,1,0:T(8,128)S(1)}) conditional(s32[]{:T(128)} %bitcast.13, (f32[8,2,256,256]{3,2,1,0:T(8,128)}, f32[256,256]{1,0:T(8,128)}, f32[4,256,256]{2,1,0:T(8,128)}, f32[2,4]{1,0:T(2,128)}, f32[8]{0:T(128)}, /*index=5*/s32[1,4,1,5]{3,2,1,0:T(1,128)}, s32[129]{0:T(256)S(1)}, ...), branch_computations={%region_0.0_spmd, %region_1.0_spmd, %region_2.0_spmd, %region_3.0_... | conditional | bytes 8 | solution.py:524
  5.9 130.3 %branch_1_fun.1 = f32[8,2,256,256]{3,2,1,0:T(8,128)S(1)} custom-call(f32[8,2,256,256]{3,2,1,0:T(8,128)} %get-tuple-element.148.rho_any, f32[256,256]{1,0:T(8,128)} %get-tuple-element.152.ham_any, f32[4,256,256]{2,1,0:T(8,128)} %get-tuple-element.156.coup_any, f32[2,4]{1,0:T(2,128)} %get-tuple-element.94.bath_ref, f32[8]{0:T(128)} %get-tuple-element.160.damp_ref, ...), custom_call_target="tpu_custom_call" | custom-call | tf_op jit(solution)/shard_map/cond/branch_1_fun/pallas_call | solution.py:524
  136.5 2.0 %copy.42 = f32[8,2,256,256]{3,2,1,0:T(8,128)} copy(f32[8,2,256,256]{3,2,1,0:T(8,128)S(1)} %get-tuple-element.126) | data formatting | bytes 8388608
